TPU v7x, 32 devices: a whole 2x2x4 slice. The times are simulated.
32 devices in a mesh: dom: 16 (over z, x, core), band: 2 (over y).
Axes of the slice: x: 2, y: 2, z: 4, core: 2. Of those that a mesh axis runs over, the one named last changes fastest.
Arguments:
- wavefun: float32 [13824, 512], P('dom', 'band')
- cell_ops: float32 [64, 343, 343], P('dom'), as said below
- cell_map: int32 [64, 343], P('dom'), may hold values from 0 to 1007, as said below
- face_list: int32 [2304], P('dom'), may hold values from 0 to 863, as said below
Outputs:
- ortho_bands: float32 [13824, 512], P('dom', 'band')
Inputs may be any that keep to these rules, and one draw needn't show every extreme that they name: `cell_map`: each row lists the 343 distinct local numbers of a cell's nodes; a number below 864 is a node of the cell's own domain, 864 + j stands for the j-th lower face node of the next domain (periodic over domains); every node of a domain belongs to some cell of that domain. `face_list`: the 144 entries of each domain are distinct node numbers of that domain. `cell_ops`: each cell's matrix is symmetric.
All inputs are finite; a program needn't handle non-finite values.
Results may differ from a plain program's by a relative error of at most 0.0001.
Values sent between devices are 32-bit elements; how exact they have to be, the bound alone decides.
A program may use at most 64 MiB of HBM per device.

v0:
```python
import jax
import jax.numpy as jnp
from jax import lax
from jax.sharding import PartitionSpec as P

DEGREE = 2
cheb_centre = 1.0
cheb_half = 1.6


def shifted(block, axis, distance):
    devices = range(lax.axis_size(axis))
    route = [((i - distance) % len(devices), i) for i in devices]
    return lax.ppermute(block, axis, route)


def on_device(wavefun, cell_ops, cell_map, face_list):
    owned_rows = wavefun.shape[0]
    block_width = wavefun.shape[1]
    flat_map = cell_map.reshape(-1)

    def local_apply(extended):
        cell_values = extended[flat_map].reshape(cell_map.shape[0], cell_map.shape[1], block_width)
        products = jnp.einsum(
            "cij,cjb->cib", cell_ops, cell_values, precision=lax.Precision.HIGHEST
        )
        return jnp.zeros_like(extended).at[flat_map].add(products.reshape(-1, block_width))

    def operate(vector):
        fetched = shifted(vector[face_list], "dom", -1)
        applied = local_apply(jnp.concatenate([vector, fetched], 0))
        returned = shifted(applied[owned_rows:], "dom", 1)
        return applied[:owned_rows].at[face_list].add(returned)

    latest = (operate(wavefun) - cheb_centre * wavefun) / cheb_half

    def advance(counter, carried):
        earlier, current = carried
        following = 2.0 * (operate(current) - cheb_centre * current) / cheb_half - earlier
        return (current, following)

    earlier, latest = lax.fori_loop(1, DEGREE, advance, (wavefun, latest))
    full_bands = lax.all_gather(latest, "band", axis=1, tiled=True)
    partial_value = jnp.einsum("nb,nc->bc", full_bands, full_bands, precision=lax.Precision.HIGHEST)
    margin = lax.psum(partial_value, "dom")
    norm_value = jnp.sqrt(jnp.sum(margin * margin) + 1e-06)
    full_width = margin.shape[0]
    offset = lax.axis_index("band") * block_width
    scaled_cols = lax.dynamic_slice_in_dim(margin, offset, block_width, 1) / norm_value
    identity_cols = lax.dynamic_slice_in_dim(
        jnp.eye(full_width, dtype=jnp.float32), offset, block_width, 1
    )
    mixing = (3.0 * identity_cols - scaled_cols) / 2.0
    return jnp.dot(full_bands, mixing, precision=lax.Precision.HIGHEST)


def solution(mesh):
    return jax.shard_map(
        on_device,
        mesh=mesh,
        in_specs=(P("dom", "band"), P("dom", None, None), P("dom", None), P("dom")),
        out_specs=P("dom", "band"),
        check_vma=False,
    )
```

profile of v0, /device:TPU:0, one launch (start us, length us, event | category | flops | bytes accessed | tf_op | source)
XLA Modules:
  0.0 234.2 jit_solution(618638592340945098)
XLA Ops:
  7.4 2.0 gather_fusion
  9.3 5.5 %collective-permute-start = (f32[144,256]{1,0:T(8,128)S(1)}, f32[144,256]{1,0:T(8,128)S(1)}, u32[]{:S(2)}, u32[]{:S(2)}) collective-permute-start(f32[144,256]{1,0:T(8,128)S(1)} %gather_fusion), channel_id=1, source_target_pairs={{2,0},{4,2},{6,4},{8,6},{10,8},{12,10},{14,12},{16,14},{18,16},{20... | collective-permute-start | bytes 442376 | tf_op jit(solution)/shard_map/ppermute | solution.py:14
  15.7 1.9 collective-permute-done
  18.7 4.6 %gather_fusion.1 = f32[1372,256]{1,0:T(8,128)} fusion(f32[1008,256]{1,0:T(8,128)S(1)} %pad_maximum_fusion, s32[2048]{0:T(1024)S(1)} %pad_clamp_fusion), kind=kCustom, calls=%fused_computation.1 | custom fusion | bytes 2815344 | tf_op jit(solution)/shard_map/gather | solution.py:23
  24.8 3.7 %fusion.4 = f32[4,343,256]{2,1,0:T(8,128)} fusion(f32[4,343,256]{2,1,0:T(8,128)S(1)} %reshape.46, f32[4,343,343]{2,0,1:T(4,128)S(1)} %copy-done), kind=kOutput, calls=%fused_computation.12 | convolution fusion | flops 1445670912 | bytes 4692240 | tf_op jit(solution)/shard_map/cij,cjb->cib/dot_general | solution.py:24
  28.5 2.6 %reshape.86 = f32[1372,256]{1,0:T(8,128)} reshape(f32[4,343,256]{2,1,0:T(8,128)} %fusion.4) | data formatting | bytes 2809856 | tf_op jit(solution)/shard_map/reshape | solution.py:27
  31.1 8.7 %scatter_custom_fusion = f32[1008,256]{1,0:T(8,128)S(1)} fusion(s32[1372]{0:T(1024)S(1)} %fusion.25, f32[1372,256]{1,0:T(8,128)} %reshape.86, f32[]{:T(128)} %constant.12.clone.1), kind=kCustom, calls=%fused_computation.29 | custom fusion | flops 351232 | bytes 1032704 | tf_op jit(solution)/shard_map/scatter-add | solution.py:27
  42.1 6.2 %collective-permute-done.1 = f32[144,256]{1,0:T(8,128)S(1)} collective-permute-done((f32[144,256]{1,0:T(8,128)S(1)}, f32[144,256]{1,0:T(8,128)S(1)}, u32[]{:S(2)}, u32[]{:S(2)}) %collective-permute-start.1) | collective-permute-done | bytes 147488 | tf_op jit(solution)/shard_map/ppermute | solution.py:14
  48.3 1.7 scatter_fusion
  50.0 2.6 %subtract_multiply_fusion = f32[864,256]{1,0:T(8,128)} fusion(f32[864,256]{1,0:T(8,128)S(1)} %scatter_fusion, f32[864,256]{1,0:T(8,128)} %param.4), kind=kLoop, calls=%fused_computation.18 | loop fusion | flops 442368 | bytes 2654208 | tf_op jit(solution)/shard_map/div | solution.py:35
  52.5 2.0 gather_fusion.2
  54.8 2.7 %collective-permute-done.2 = f32[144,256]{1,0:T(8,128)S(1)} collective-permute-done((f32[144,256]{1,0:T(8,128)S(1)}, f32[144,256]{1,0:T(8,128)S(1)}, u32[]{:S(2)}, u32[]{:S(2)}) %collective-permute-start.2) | collective-permute-done | bytes 147488 | tf_op jit(solution)/shard_map/while/body/eval_jaxpr/ppermute | solution.py:14
  58.7 4.6 %gather_fusion.3 = f32[1372,256]{1,0:T(8,128)} fusion(f32[1008,256]{1,0:T(8,128)S(1)} %pad_maximum_fusion.1, s32[2048]{0:T(1024)S(1)} %pad_clamp_fusion), kind=kCustom, calls=%fused_computation.3 | custom fusion | bytes 2815344 | tf_op jit(solution)/shard_map/while/body/eval_jaxpr/gather | solution.py:23
  64.7 3.7 %fusion.7 = f32[4,343,256]{2,1,0:T(8,128)} fusion(f32[4,343,256]{2,1,0:T(8,128)S(1)} %reshape.48, f32[4,343,343]{2,0,1:T(4,128)S(1)} %copy-done), kind=kOutput, calls=%fused_computation.13 | convolution fusion | flops 1445670912 | bytes 4692240 | tf_op jit(solution)/shard_map/while/body/eval_jaxpr/cij,cjb->cib/dot_general | solution.py:24
  68.4 2.6 %reshape.102 = f32[1372,256]{1,0:T(8,128)} reshape(f32[4,343,256]{2,1,0:T(8,128)} %fusion.7) | data formatting | bytes 2809856 | tf_op jit(solution)/shard_map/while/body/eval_jaxpr/reshape | solution.py:27
  71.0 8.7 %scatter_custom_fusion.2 = f32[1008,256]{1,0:T(8,128)S(1)} fusion(s32[1372]{0:T(1024)S(1)} %fusion.25, f32[1372,256]{1,0:T(8,128)} %reshape.102, f32[]{:T(128)} %constant.12.clone.1), kind=kCustom, calls=%fused_computation.27 | custom fusion | flops 351232 | bytes 1032704 | tf_op jit(solution)/shard_map/while/body/eval_jaxpr/scatter-add | solution.py:27
  80.8 6.4 %collective-permute-done.3 = f32[144,256]{1,0:T(8,128)S(1)} collective-permute-done((f32[144,256]{1,0:T(8,128)S(1)}, f32[144,256]{1,0:T(8,128)S(1)}, u32[]{:S(2)}, u32[]{:S(2)}) %collective-permute-start.3) | collective-permute-done | bytes 147488 | tf_op jit(solution)/shard_map/while/body/eval_jaxpr/ppermute | solution.py:14
  87.3 3.3 %scatter_fusion.1 = f32[864,256]{1,0:T(8,128)} fusion(f32[864,256]{1,0:T(8,128)} %slice.28, s32[144]{0:T(256)S(1)} %compare_select_fusion.1, f32[144,256]{1,0:T(8,128)S(1)} %collective-permute-done.3), kind=kCustom, calls=%fused_computation.7 | custom fusion | flops 36864 | bytes 442944 | tf_op jit(solution)/shard_map/while/body/eval_jaxpr/scatter-add | solution.py:33
  90.6 2.6 %multiply_subtract_fusion = f32[864,256]{1,0:T(8,128)} fusion(f32[864,256]{1,0:T(8,128)} %param.4, f32[864,256]{1,0:T(8,128)} %scatter_fusion.1, f32[864,256]{1,0:T(8,128)S(1)} %copy-done.2), kind=kLoop, calls=%fused_computation.17 | loop fusion | flops 1105920 | bytes 3538944 | tf_op jit(solution)/shard_map/while/body/eval_jaxpr/sub | solution.py:39
  93.5 26.6 %all-gather.2.cloned.1.call-done = f32[864,512]{1,0:T(8,128)} async-done(((f32[864,256]{1,0:T(8,128)}), f32[864,512]{1,0:T(8,128)}) %all-gather.2.cloned.1.call-update) | async-done | bytes 1769488 | tf_op jit(solution)/shard_map/all_gather | solution.py:43
  120.0 6.5 %fusion.29 = f32[512,512]{1,0:T(8,128)} fusion(f32[864,512]{1,0:T(8,128)} %all-gather.2.cloned.1.call-done), kind=kOutput, calls=%fused_computation.43 | convolution fusion | flops 2717908992 | bytes 2818048 | tf_op jit(solution)/shard_map/nb,nc->bc/dot_general | solution.py:44
  126.6 93.8 %all-reduce.2.cloned.1.call-done = f32[512,512]{1,0:T(8,128)} async-done(((f32[512,512]{1,0:T(8,128)}), f32[512,512]{1,0:T(8,128)}) %all-reduce.2.cloned.1.call-update) | async-done | bytes 1048592 | tf_op jit(solution)/shard_map/psum | solution.py:45
  220.5 2.1 multiply_reduce_fusion
  223.2 4.1 %fusion.10 = f32[864,256]{1,0:T(8,128)} fusion(f32[864,512]{1,0:T(8,128)} %all-gather.2.cloned.1.call-done, f32[512,512]{1,0:T(8,128)} %all-reduce.2.cloned.1.call-done, s32[]{:T(128)S(6)} %select_n.27, f32[]{:T(128)S(6)} %sqrt.3), kind=kOutput, calls=%fused_computation.20 | convolution fusion | flops 1359872000 | bytes 3180032 | tf_op jit(solution)/shard_map/dot_general | solution.py:54
  (28 shorter events, 10.9 us)
Async XLA Ops:
  6.5 18.3 %copy-start = (f32[4,343,343]{2,0,1:T(4,128)S(1)}, f32[4,343,343]{2,0,1:T(4,128)}, u32[]{:S(2)}) copy-start(f32[4,343,343]{2,0,1:T(4,128)} %param.5) | copy-start | bytes 5647156
  6.5 113.5 %all-gather.2.cloned.1.call-start = ((), (), s32[]{:S(2)}) async-start(), calls=%async_computation | async-start | bytes 2654208 | tf_op jit(solution)/shard_map/all_gather | solution.py:43
  9.3 8.2 %collective-permute-start = (f32[144,256]{1,0:T(8,128)S(1)}, f32[144,256]{1,0:T(8,128)S(1)}, u32[]{:S(2)}, u32[]{:S(2)}) collective-permute-start(f32[144,256]{1,0:T(8,128)S(1)} %gather_fusion), channel_id=1, source_target_pairs={{2,0},{4,2},{6,4},{8,6},{10,8},{12,10},{14,12},{16,14},{18,16},{20... | collective-permute-start | bytes 442376 | tf_op jit(solution)/shard_map/ppermute | solution.py:14
  39.9 1.0 copy-start.3
  40.8 7.4 %collective-permute-start.1 = (f32[144,256]{1,0:T(8,128)S(1)}, f32[144,256]{1,0:T(8,128)S(1)}, u32[]{:S(2)}, u32[]{:S(2)}) collective-permute-start(f32[144,256]{1,0:T(8,128)S(1)} %slice.27), channel_id=1, source_target_pairs={{30,0},{0,2},{2,4},{4,6},{6,8},{8,10},{10,12},{12,14},{14,16},{16,... | collective-permute-start | bytes 442376 | tf_op jit(solution)/shard_map/ppermute | solution.py:14
  50.0 4.5 %copy-start.1 = (f32[864,256]{1,0:T(8,128)}, f32[864,256]{1,0:T(8,128)S(1)}, u32[]{:S(2)}) copy-start(f32[864,256]{1,0:T(8,128)S(1)} %scatter_fusion) | copy-start | bytes 2654212
  54.5 2.9 %collective-permute-start.2 = (f32[144,256]{1,0:T(8,128)S(1)}, f32[144,256]{1,0:T(8,128)S(1)}, u32[]{:S(2)}, u32[]{:S(2)}) collective-permute-start(f32[144,256]{1,0:T(8,128)S(1)} %gather_fusion.2), channel_id=1, source_target_pairs={{2,0},{4,2},{6,4},{8,6},{10,8},{12,10},{14,12},{16,14},{18,16},{20... | collective-permute-start | bytes 442376 | tf_op jit(solution)/shard_map/while/body/eval_jaxpr/ppermute | solution.py:14
  79.8 7.5 %collective-permute-start.3 = (f32[144,256]{1,0:T(8,128)S(1)}, f32[144,256]{1,0:T(8,128)S(1)}, u32[]{:S(2)}, u32[]{:S(2)}) collective-permute-start(f32[144,256]{1,0:T(8,128)S(1)} %slice.29), channel_id=1, source_target_pairs={{30,0},{0,2},{2,4},{4,6},{6,8},{8,10},{10,12},{12,14},{14,16},{16,... | collective-permute-start | bytes 442376 | tf_op jit(solution)/shard_map/while/body/eval_jaxpr/ppermute | solution.py:14
  80.8 9.8 %copy-start.2 = (f32[864,256]{1,0:T(8,128)S(1)}, f32[864,256]{1,0:T(8,128)}, u32[]{:S(2)}) copy-start(f32[864,256]{1,0:T(8,128)} %copy-done.1) | copy-start | bytes 2654212
  93.2 127.3 %all-reduce.2.cloned.1.call-start = ((), (), s32[]{:S(2)}) async-start(), calls=%async_computation.1 | async-start | bytes 2097152 | tf_op jit(solution)/shard_map/psum | solution.py:45
Sparse Core Ops, SparseCore 0:
  93.3 26.6 all-gather.1
  126.7 93.6 all-reduce.1
where the time goes:
time: 235 us; the launch traced here: 234 us
  waiting for transfers between devices  138 us (59%)
  other arithmetic  33.1 us (14%)
  local copies, waits for them, and re-layouts  25.3 us (11%)
  matrix products  18 us (8%)
  between operations  14.2 us (6%)
  starting transfers between devices  6.06 us (3%)
    psum x1, waiting for transfers between devices, on_device(): margin = lax.psum(partial_value, 'dom')  93.8 us
    all_gather x1, waiting for transfers between devices, on_device(): full_bands = lax.all_gather(latest, 'band', axis=1, tiled=True)  26.6 us
    scatter-add x2, other arithmetic, local_apply(): jnp.zeros_like(extended).at[flat_map].add(products.reshape(-1, block_width))  17.4 us
    ppermute x4, waiting for transfers between devices, shifted(): return lax.ppermute(block, axis, route)  17.1 us
    gather x2, local copies, waits for them, and re-layouts, local_apply(): extended[flat_map]  9.14 us
    dot_general x2, matrix products, local_apply(): jnp.einsum('cij,cjb->cib', cell_ops, cell_values, precision=lax.Precision...  7.36 us
    dot_general x1, matrix products, on_device(): jnp.einsum('nb,nc->bc', full_bands, full_bands, precision=lax.Precision.H...  6.54 us
    ppermute x4, starting transfers between devices, shifted(): return lax.ppermute(block, axis, route)  5.8 us
  transfers between devices with their start and end apart: 6, of which 6 were waited for; matrix products, arithmetic and copies ran while one was open for 1% of the time, Pallas kernels for 0%

commit v1 on v0

--- a/solution.py
+++ b/solution.py
@@ -1,3 +1,4 @@
+import functools
 import jax
 import jax.numpy as jnp
 from jax import lax
@@ -6,6 +7,14 @@
 DEGREE = 2
 cheb_centre = 1.0
 cheb_half = 1.6
+
+
+def draft_shifts_all(state, ax_name):
+    w_next = jnp.sum(lax.all_gather(state, axis_name=ax_name), 0)
+    return w_next
+
+
+_start_panel = functools.partial(draft_shifts_all, ax_name="dom")
 
 
 def shifted(block, axis, distance):
@@ -42,7 +51,7 @@
     earlier, latest = lax.fori_loop(1, DEGREE, advance, (wavefun, latest))
     full_bands = lax.all_gather(latest, "band", axis=1, tiled=True)
     partial_value = jnp.einsum("nb,nc->bc", full_bands, full_bands, precision=lax.Precision.HIGHEST)
-    margin = lax.psum(partial_value, "dom")
+    margin = _start_panel(partial_value)
     norm_value = jnp.sqrt(jnp.sum(margin * margin) + 1e-06)
     full_width = margin.shape[0]
     offset = lax.axis_index("band") * block_width

time: 235 us -> 274 us (1.17)
  waiting for transfers between devices: 138 us -> 170 us
  other arithmetic: 33.1 us -> 39.8 us
    all_gather x0 -> x1, waiting for transfers between devices: none -> 127 us  [draft_shifts_all(): w_next = jnp.sum(lax.all_gather(state, axis_name=ax_name), 0)]
    psum x1 -> x0, waiting for transfers between devices: 93.8 us -> none  [on_device(): margin = lax.psum(partial_value, 'dom')]
    reduce_sum x0 -> x1, other arithmetic: none -> 7.95 us  [draft_shifts_all(): w_next = jnp.sum(lax.all_gather(state, axis_name=ax_name), 0)]
where the time goes in v1:
time: 274 us; the launch traced here: 273 us
  waiting for transfers between devices  170 us (62%)
  other arithmetic  39.8 us (15%)
  local copies, waits for them, and re-layouts  25.3 us (9%)
  matrix products  17.8 us (6%)
  between operations  14.2 us (5%)
  starting transfers between devices  6.06 us (2%)
    all_gather x1, waiting for transfers between devices, draft_shifts_all(): w_next = jnp.sum(lax.all_gather(state, axis_name=ax_name), 0)  127 us
    all_gather x1, waiting for transfers between devices, on_device(): full_bands = lax.all_gather(latest, 'band', axis=1, tiled=True)  26.6 us
    scatter-add x2, other arithmetic, local_apply(): jnp.zeros_like(extended).at[flat_map].add(products.reshape(-1, block_width))  17.4 us
    ppermute x4, waiting for transfers between devices, shifted(): return lax.ppermute(block, axis, route)  17.1 us
    gather x2, local copies, waits for them, and re-layouts, local_apply(): extended[flat_map]  9.14 us
    reduce_sum x1, other arithmetic, draft_shifts_all(): w_next = jnp.sum(lax.all_gather(state, axis_name=ax_name), 0)  7.95 us
    dot_general x2, matrix products, local_apply(): jnp.einsum('cij,cjb->cib', cell_ops, cell_values, precision=lax.Precision...  7.36 us
    dot_general x1, matrix products, on_device(): jnp.einsum('nb,nc->bc', full_bands, full_bands, precision=lax.Precision.H...  6.48 us
  transfers between devices with their start and end apart: 6, of which 6 were waited for; matrix products, arithmetic and copies ran while one was open for 1% of the time, Pallas kernels for 0%

profile of v1, /device:TPU:0, one launch (start us, length us, event | category | flops | bytes accessed | tf_op | source)
XLA Modules:
  0.0 273.5 jit_solution(15837022647197267030)
XLA Ops:
  7.4 2.0 gather_fusion
  9.3 5.5 %collective-permute-start = (f32[144,256]{1,0:T(8,128)S(1)}, f32[144,256]{1,0:T(8,128)S(1)}, u32[]{:S(2)}, u32[]{:S(2)}) collective-permute-start(f32[144,256]{1,0:T(8,128)S(1)} %gather_fusion), channel_id=1, source_target_pairs={{2,0},{4,2},{6,4},{8,6},{10,8},{12,10},{14,12},{16,14},{18,16},{20... | collective-permute-start | bytes 442376 | tf_op jit(solution)/shard_map/ppermute | solution.py:23
  15.7 1.9 collective-permute-done
  18.7 4.6 %gather_fusion.1 = f32[1372,256]{1,0:T(8,128)} fusion(f32[1008,256]{1,0:T(8,128)S(1)} %pad_maximum_fusion, s32[2048]{0:T(1024)S(1)} %pad_clamp_fusion), kind=kCustom, calls=%fused_computation.1 | custom fusion | bytes 2815344 | tf_op jit(solution)/shard_map/gather | solution.py:32
  24.8 3.7 %fusion.4 = f32[4,343,256]{2,1,0:T(8,128)} fusion(f32[4,343,256]{2,1,0:T(8,128)S(1)} %reshape.46, f32[4,343,343]{2,0,1:T(4,128)S(1)} %copy-done), kind=kOutput, calls=%fused_computation.12 | convolution fusion | flops 1445670912 | bytes 4692240 | tf_op jit(solution)/shard_map/cij,cjb->cib/dot_general | solution.py:33
  28.5 2.6 reshape.86
  31.1 8.7 %scatter_custom_fusion = f32[1008,256]{1,0:T(8,128)S(1)} fusion(s32[1372]{0:T(1024)S(1)} %fusion.25, f32[1372,256]{1,0:T(8,128)} %reshape.86, f32[]{:T(128)} %constant.12.clone.1), kind=kCustom, calls=%fused_computation.29 | custom fusion | flops 351232 | bytes 1032704 | tf_op jit(solution)/shard_map/scatter-add | solution.py:36
  42.1 6.2 %collective-permute-done.1 = f32[144,256]{1,0:T(8,128)S(1)} collective-permute-done((f32[144,256]{1,0:T(8,128)S(1)}, f32[144,256]{1,0:T(8,128)S(1)}, u32[]{:S(2)}, u32[]{:S(2)}) %collective-permute-start.1) | collective-permute-done | bytes 147488 | tf_op jit(solution)/shard_map/ppermute | solution.py:23
  48.3 1.7 scatter_fusion
  50.0 2.6 subtract_multiply_fusion
  52.5 2.0 gather_fusion.2
  54.8 2.7 collective-permute-done.2
  58.7 4.6 %gather_fusion.3 = f32[1372,256]{1,0:T(8,128)} fusion(f32[1008,256]{1,0:T(8,128)S(1)} %pad_maximum_fusion.1, s32[2048]{0:T(1024)S(1)} %pad_clamp_fusion), kind=kCustom, calls=%fused_computation.3 | custom fusion | bytes 2815344 | tf_op jit(solution)/shard_map/while/body/eval_jaxpr/gather | solution.py:32
  64.7 3.7 %fusion.7 = f32[4,343,256]{2,1,0:T(8,128)} fusion(f32[4,343,256]{2,1,0:T(8,128)S(1)} %reshape.48, f32[4,343,343]{2,0,1:T(4,128)S(1)} %copy-done), kind=kOutput, calls=%fused_computation.13 | convolution fusion | flops 1445670912 | bytes 4692240 | tf_op jit(solution)/shard_map/while/body/eval_jaxpr/cij,cjb->cib/dot_general | solution.py:33
  68.4 2.6 reshape.102
  71.0 8.7 %scatter_custom_fusion.2 = f32[1008,256]{1,0:T(8,128)S(1)} fusion(s32[1372]{0:T(1024)S(1)} %fusion.25, f32[1372,256]{1,0:T(8,128)} %reshape.102, f32[]{:T(128)} %constant.12.clone.1), kind=kCustom, calls=%fused_computation.27 | custom fusion | flops 351232 | bytes 1032704 | tf_op jit(solution)/shard_map/while/body/eval_jaxpr/scatter-add | solution.py:36
  80.8 6.4 %collective-permute-done.3 = f32[144,256]{1,0:T(8,128)S(1)} collective-permute-done((f32[144,256]{1,0:T(8,128)S(1)}, f32[144,256]{1,0:T(8,128)S(1)}, u32[]{:S(2)}, u32[]{:S(2)}) %collective-permute-start.3) | collective-permute-done | bytes 147488 | tf_op jit(solution)/shard_map/while/body/eval_jaxpr/ppermute | solution.py:23
  87.3 3.3 %scatter_fusion.1 = f32[864,256]{1,0:T(8,128)} fusion(f32[864,256]{1,0:T(8,128)} %slice.28, s32[144]{0:T(256)S(1)} %compare_select_fusion.1, f32[144,256]{1,0:T(8,128)S(1)} %collective-permute-done.3), kind=kCustom, calls=%fused_computation.7 | custom fusion | flops 36864 | bytes 442944 | tf_op jit(solution)/shard_map/while/body/eval_jaxpr/scatter-add | solution.py:42
  90.6 2.6 multiply_subtract_fusion
  93.5 26.6 %all-gather.4.cloned.1.call-done = f32[864,512]{1,0:T(8,128)} async-done(((f32[864,256]{1,0:T(8,128)}), f32[864,512]{1,0:T(8,128)}) %all-gather.4.cloned.1.call-update) | async-done | bytes 1769488 | tf_op jit(solution)/shard_map/all_gather | solution.py:52
  120.0 6.5 %fusion.29 = f32[512,512]{1,0:T(8,128)} fusion(f32[864,512]{1,0:T(8,128)} %all-gather.4.cloned.1.call-done), kind=kOutput, calls=%fused_computation.43 | convolution fusion | flops 2717908992 | bytes 2818048 | tf_op jit(solution)/shard_map/nb,nc->bc/dot_general | solution.py:53
  126.5 126.6 %all-gather.6.cloned.1.call-done = f32[8192,512]{1,0:T(8,128)} async-done(((f32[512,512]{1,0:T(8,128)}), f32[8192,512]{1,0:T(8,128)}) %all-gather.6.cloned.1.call-update) | async-done | bytes 16777232 | tf_op jit(solution)/shard_map/all_gather | solution.py:13
  253.1 8.0 %reduce_sum.18 = f32[512,512]{1,0:T(8,128)S(1)} reduce(f32[16,512,512]{2,1,0:T(8,128)} %bitcast.10, f32[]{:T(128)} %constant.12.clone.1), dimensions={0}, to_apply=%region_4.5 | reduce | flops 3932160 | bytes 17825796 | tf_op jit(solution)/shard_map/reduce_sum | solution.py:13
  262.6 4.0 %fusion.10 = f32[864,256]{1,0:T(8,128)} fusion(f32[864,512]{1,0:T(8,128)} %all-gather.4.cloned.1.call-done, f32[512,512]{1,0:T(8,128)S(1)} %reduce_sum.18, s32[]{:T(128)S(6)} %select_n.27, f32[]{:T(128)S(6)} %sqrt.3), kind=kOutput, calls=%fused_computation.20 | convolution fusion | flops 1359872000 | bytes 3180032 | tf_op jit(solution)/shard_map/dot_general | solution.py:63
  (29 shorter events, 11.8 us)
Async XLA Ops:
  6.5 18.3 %copy-start = (f32[4,343,343]{2,0,1:T(4,128)S(1)}, f32[4,343,343]{2,0,1:T(4,128)}, u32[]{:S(2)}) copy-start(f32[4,343,343]{2,0,1:T(4,128)} %param.5) | copy-start | bytes 5647156
  6.5 113.5 %all-gather.4.cloned.1.call-start = ((), (), s32[]{:S(2)}) async-start(), calls=%async_computation | async-start | bytes 2654208 | tf_op jit(solution)/shard_map/all_gather | solution.py:52
  9.3 8.2 %collective-permute-start = (f32[144,256]{1,0:T(8,128)S(1)}, f32[144,256]{1,0:T(8,128)S(1)}, u32[]{:S(2)}, u32[]{:S(2)}) collective-permute-start(f32[144,256]{1,0:T(8,128)S(1)} %gather_fusion), channel_id=1, source_target_pairs={{2,0},{4,2},{6,4},{8,6},{10,8},{12,10},{14,12},{16,14},{18,16},{20... | collective-permute-start | bytes 442376 | tf_op jit(solution)/shard_map/ppermute | solution.py:23
  39.9 1.0 copy-start.3
  40.8 7.4 %collective-permute-start.1 = (f32[144,256]{1,0:T(8,128)S(1)}, f32[144,256]{1,0:T(8,128)S(1)}, u32[]{:S(2)}, u32[]{:S(2)}) collective-permute-start(f32[144,256]{1,0:T(8,128)S(1)} %slice.27), channel_id=1, source_target_pairs={{30,0},{0,2},{2,4},{4,6},{6,8},{8,10},{10,12},{12,14},{14,16},{16,... | collective-permute-start | bytes 442376 | tf_op jit(solution)/shard_map/ppermute | solution.py:23
  50.0 4.5 %copy-start.1 = (f32[864,256]{1,0:T(8,128)}, f32[864,256]{1,0:T(8,128)S(1)}, u32[]{:S(2)}) copy-start(f32[864,256]{1,0:T(8,128)S(1)} %scatter_fusion) | copy-start | bytes 2654212
  54.5 2.9 %collective-permute-start.2 = (f32[144,256]{1,0:T(8,128)S(1)}, f32[144,256]{1,0:T(8,128)S(1)}, u32[]{:S(2)}, u32[]{:S(2)}) collective-permute-start(f32[144,256]{1,0:T(8,128)S(1)} %gather_fusion.2), channel_id=1, source_target_pairs={{2,0},{4,2},{6,4},{8,6},{10,8},{12,10},{14,12},{16,14},{18,16},{20... | collective-permute-start | bytes 442376 | tf_op jit(solution)/shard_map/while/body/eval_jaxpr/ppermute | solution.py:23
  79.8 7.5 %collective-permute-start.3 = (f32[144,256]{1,0:T(8,128)S(1)}, f32[144,256]{1,0:T(8,128)S(1)}, u32[]{:S(2)}, u32[]{:S(2)}) collective-permute-start(f32[144,256]{1,0:T(8,128)S(1)} %slice.29), channel_id=1, source_target_pairs={{30,0},{0,2},{2,4},{4,6},{6,8},{8,10},{10,12},{12,14},{14,16},{16,... | collective-permute-start | bytes 442376 | tf_op jit(solution)/shard_map/while/body/eval_jaxpr/ppermute | solution.py:23
  80.8 9.8 %copy-start.2 = (f32[864,256]{1,0:T(8,128)S(1)}, f32[864,256]{1,0:T(8,128)}, u32[]{:S(2)}) copy-start(f32[864,256]{1,0:T(8,128)} %copy-done.1) | copy-start | bytes 2654212
  93.2 159.9 %all-gather.6.cloned.1.call-start = ((), (), s32[]{:S(2)}) async-start(), calls=%async_computation.1 | async-start | bytes 17825792 | tf_op jit(solution)/shard_map/all_gather | solution.py:13
Sparse Core Ops, SparseCore 0:
  93.3 26.6 all-gather.3
  126.7 126.4 all-gather.5
